TPU v7x, 32 devices: a whole 2x2x4 slice. The times are simulated.
32 devices in a mesh: groups: 2 (over x), slab: 16 (over z, y, core).
Axes of the slice: x: 2, y: 2, z: 4, core: 2. Of those that a mesh axis runs over, the one named last changes fastest.
Arguments:
- activations: bfloat16 [2048, 65536], P(('groups', 'slab')), parts along dimension 0, may hold values from 0 to 4
- weights: bfloat16 [6, 2, 512, 128, 128], P(None, None, 'slab'), may hold values from -0.5 to 0.5
- biases: float32 [6, 65536], P(None, 'slab'), may hold values from -1 to 0.5
- columns: int32 [6, 512], P(None, 'slab'), may hold values from 0 to 31
Outputs:
- features: bfloat16 [2048, 65536], P(('groups', 'slab')), parts along dimension 0
There are 2 independent parts, one for each index of `groups`. A program takes and returns all parts, laid end to end along the dimension named above; an argument that names none is the same for every part. Nothing has to cross between parts.
Inputs may be any that keep to these rules, and one draw needn't show every extreme that they name: columns name a block within a group of 32 consecutive blocks.
All inputs are finite; a program needn't handle non-finite values.
Results may differ from a plain program's by a relative error of at most 0.0072.
Values may be sent and summed in bfloat16 or wider, within the bound.
No kernel may reach another device: no remote copies, remote signals or barrier semaphores. Data moves between devices by JAX's collectives and lax.ppermute only.
A program may use at most 128 MiB of HBM per device.

v0:
```python
import jax
import jax.numpy as jnp
from jax import lax
from jax.sharding import PartitionSpec as P

ceiling = 4.0


def from_partner(block, axis, bit):
    count = lax.axis_size(axis)
    route = []
    for low in range(count):
        high = low | 1 << bit
        if high != low and high < count:
            route += [(low, high), (high, low)]
    return lax.ppermute(block, axis, route)


def section_bit(section, remote, log_count):
    return (remote - 1 - section) * (log_count - 1) // (remote - 1)


def local(activations, weights, biases, columns):
    slab_count = lax.axis_size("slab")
    log_count = slab_count.bit_length() - 1
    layer_count = weights.shape[0]
    per_device = weights.shape[2]
    block_width = weights.shape[3]
    local_rows = activations.shape[0]
    remote = (layer_count + 1) // 2
    grouped = activations.reshape(local_rows, slab_count, per_device * block_width)
    stride = 1 << section_bit(0, remote, log_count)
    flipped = grouped.reshape(
        local_rows, slab_count // (2 * stride), 2, stride, per_device * block_width
    )
    flipped = flipped[:, :, ::-1].reshape(local_rows, slab_count, per_device * block_width)
    paired = jnp.stack([grouped, flipped], axis=2)
    arrived = lax.all_to_all(paired, "slab", split_axis=1, concat_axis=0, tiled=True)
    current = arrived[:, 0, 0].reshape(-1, per_device, block_width)
    first_cross = arrived[:, 0, 1].reshape(-1, per_device, block_width)
    for layer_index in range(layer_count):
        if layer_index % 2 == 0:
            if layer_index == 0 and first_cross is not None:
                source = first_cross
            else:
                source = from_partner(
                    current, "slab", section_bit(layer_index // 2, remote, log_count)
                )
        else:
            source = current
        crossing = jnp.take(source, columns[layer_index], axis=1)
        summed = jnp.einsum(
            "rkb,kbc->rkc", current, weights[layer_index, 0], preferred_element_type=jnp.float32
        )
        summed = summed + jnp.einsum(
            "rkb,kbc->rkc", crossing, weights[layer_index, 1], preferred_element_type=jnp.float32
        )
        summed = summed + biases[layer_index].reshape(per_device, block_width)
        current = jnp.clip(summed, 0.0, ceiling).astype(jnp.bfloat16)
    flattened = current.reshape(current.shape[0], per_device * block_width)
    return lax.all_to_all(flattened, "slab", split_axis=0, concat_axis=1, tiled=True)


def solution(mesh):
    placed = (
        P(("groups", "slab"), None),
        P(None, None, "slab", None, None),
        P(None, "slab"),
        P(None, "slab"),
    )
    return jax.shard_map(
        local, mesh=mesh, in_specs=placed, out_specs=P(("groups", "slab"), None), check_vma=False
    )
```

profile of v0, /device:TPU:1, one launch (start us, length us, event | category | flops | bytes accessed | tf_op | source)
XLA Modules:
  0.0 1066.5 jit_solution(5412748452448401006)
XLA Ops:
  0.0 12.1 %copy.28 = bf16[8,8,16,4096]{3,2,1,0:T(8,128)(2,1)} copy(bf16[8,8,16,4096]{3,1,2,0:T(8,128)(2,1)} %bitcast.134) | data formatting | bytes 16777216
  12.1 7.7 reverse_bitcast_fusion
  19.9 8.0 pad_maximum_fusion
  27.9 21.4 %copy.18 = bf16[64,16,2,4096]{3,0,2,1:T(8,128)(2,1)} copy(bf16[64,16,2,4096]{3,1,0,2:T(8,128)(2,1)S(1)} %pad_maximum_fusion) | data formatting | bytes 33554432 | tf_op jit(solution)/shard_map/stack | solution.py:37
  49.2 0.0 copy-start.2
  49.2 0.0 copy-start
  49.2 8.1 all-to-all-start
  57.4 0.0 copy-done.2
  57.4 0.5 compare_and_fusion
  57.9 0.0 copy-done
  57.9 0.7 fusion.79
  58.6 295.9 %all-to-all-done = bf16[64,16,2,4096]{3,0,2,1:T(8,128)(2,1)} async-done(((bf16[64,16,2,4096]{3,0,2,1:T(8,128)(2,1)}), bf16[64,16,2,4096]{3,0,2,1:T(8,128)(2,1)}, u32[]{:S(2)}, u32[]{:S(2)}) %all-to-all-start) | async-done | bytes 16777248 | tf_op jit(solution)/shard_map/all_to_all | solution.py:38
  354.5 8.3 copy.19
  362.7 6.4 fusion.78
  369.2 12.0 %copy.22 = bf16[1024,1,1,4096]{0,3,2,1:T(8,128)(2,1)} copy(bf16[1024,1,1,4096]{3,0,2,1:T(8,128)(2,1)} %get-tuple-element.18) | data formatting | bytes 16777216 | tf_op jit(solution)/shard_map/slice | solution.py:40
  381.1 11.4 %copy.23 = bf16[1024,32,128]{2,0,1:T(8,128)(2,1)} copy(bf16[1024,32,128]{0,2,1:T(8,128)(2,1)} %bitcast.132) | data formatting | bytes 16777216 | tf_op jit(solution)/shard_map/reshape;squeeze | solution.py:40
  392.5 11.9 %copy.20 = bf16[1024,1,1,4096]{0,3,2,1:T(8,128)(2,1)} copy(bf16[1024,1,1,4096]{3,0,2,1:T(8,128)(2,1)} %get-tuple-element.19) | data formatting | bytes 16777216 | tf_op jit(solution)/shard_map/slice | solution.py:39
  404.4 8.4 gather_fusion
  412.8 11.8 %fusion.58 = f32[32,1024,128]{2,1,0:T(8,128)} fusion(bf16[1024,32,128]{0,2,1:T(8,128)(2,1)} %bitcast.131, bf16[6,2,32,128,128]{4,3,2,1,0:T(8,128)(2,1)} %param.7), kind=kOutput, calls=%fused_computation.60 | convolution fusion | flops 1073741824 | bytes 26214400 | tf_op jit(solution)/shard_map/rkb,kbc->rkc/dot_general | solution.py:52
  424.6 13.5 %fusion.18 = bf16[1024,32,128]{2,0,1:T(8,128)(2,1)} fusion(f32[32,128]{1,0:T(8,128)S(1)} %bitcast.140, f32[32,1024,128]{2,1,0:T(8,128)} %fusion.58, bf16[32,1024,128]{2,1,0:T(8,128)(2,1)} %gather_fusion, pred[32]{0:T(512)(128)(4,1)S(1)} %get-tuple-element.32, bf16[6,2,32,128,128]{4,3,2,1,0:T(8,128)(2,1)} %param.7), kind=kOutput, calls=%fused_computation.32 | convolution fusion | flops 1094713344 | bytes 34619424 | tf_op jit(solution)/shard_map/rkb,kbc->rkc/dot_general | solution.py:55
  438.2 11.7 %fusion.55 = f32[32,1024,128]{2,1,0:T(8,128)} fusion(bf16[1024,32,128]{2,0,1:T(8,128)(2,1)} %fusion.18, bf16[6,2,32,128,128]{4,3,2,1,0:T(8,128)(2,1)} %param.7), kind=kOutput, calls=%fused_computation.57 | convolution fusion | flops 1073741824 | bytes 26214400 | tf_op jit(solution)/shard_map/rkb,kbc->rkc/dot_general | solution.py:52
  449.8 8.4 gather_fusion.1
  458.2 13.7 %fusion.21 = bf16[1024,32,128]{2,0,1:T(8,128)(2,1)} fusion(f32[32,128]{1,0:T(8,128)S(1)} %bitcast.139, f32[32,1024,128]{2,1,0:T(8,128)} %fusion.55, bf16[32,1024,128]{2,1,0:T(8,128)(2,1)} %gather_fusion.1, pred[32]{0:T(512)(128)(4,1)S(1)} %get-tuple-element.30, bf16[6,2,32,128,128]{4,3,2,1,0:T(8,128)(2,1)} %param.7), kind=kOutput, calls=%fused_computation.33 | convolution fusion | flops 1094713344 | bytes 34619424 | tf_op jit(solution)/shard_map/rkb,kbc->rkc/dot_general | solution.py:55
  471.9 22.8 %collective-permute-start = (bf16[1024,32,128]{2,0,1:T(8,128)(2,1)}, bf16[1024,32,128]{2,0,1:T(8,128)(2,1)}, u32[]{:S(2)}, u32[]{:S(2)}) collective-permute-start(bf16[1024,32,128]{2,0,1:T(8,128)(2,1)} %fusion.21), channel_id=1, source_target_pairs={{0,2},{2,0},{1,3},{3,1},{4,6},{6,4},{5,7},{7,5},{8,10},{10,8},{9,1... | collective-permute-start | bytes 25165832 | tf_op jit(solution)/shard_map/ppermute | solution.py:16
  494.7 11.7 %fusion.52 = f32[32,1024,128]{2,1,0:T(8,128)} fusion(bf16[1024,32,128]{2,0,1:T(8,128)(2,1)} %fusion.21, bf16[6,2,32,128,128]{4,3,2,1,0:T(8,128)(2,1)} %param.7), kind=kOutput, calls=%fused_computation.54 | convolution fusion | flops 1073741824 | bytes 26214400 | tf_op jit(solution)/shard_map/rkb,kbc->rkc/dot_general | solution.py:52
  506.4 169.1 %collective-permute-done = bf16[1024,32,128]{2,0,1:T(8,128)(2,1)} collective-permute-done((bf16[1024,32,128]{2,0,1:T(8,128)(2,1)}, bf16[1024,32,128]{2,0,1:T(8,128)(2,1)}, u32[]{:S(2)}, u32[]{:S(2)}) %collective-permute-start) | collective-permute-done | bytes 8388640 | tf_op jit(solution)/shard_map/ppermute | solution.py:16
  675.5 8.6 gather_fusion.2
  684.1 13.5 %fusion.24 = bf16[1024,32,128]{2,0,1:T(8,128)(2,1)} fusion(f32[32,128]{1,0:T(8,128)S(1)} %bitcast.138, f32[32,1024,128]{2,1,0:T(8,128)} %fusion.52, bf16[32,1024,128]{2,1,0:T(8,128)(2,1)} %gather_fusion.2, pred[32]{0:T(512)(128)(4,1)S(1)} %get-tuple-element.28, bf16[6,2,32,128,128]{4,3,2,1,0:T(8,128)(2,1)} %param.7), kind=kOutput, calls=%fused_computation.34 | convolution fusion | flops 1094713344 | bytes 34619424 | tf_op jit(solution)/shard_map/rkb,kbc->rkc/dot_general | solution.py:55
  697.6 11.7 %fusion.49 = f32[32,1024,128]{2,1,0:T(8,128)} fusion(bf16[1024,32,128]{2,0,1:T(8,128)(2,1)} %fusion.24, bf16[6,2,32,128,128]{4,3,2,1,0:T(8,128)(2,1)} %param.7), kind=kOutput, calls=%fused_computation.51 | convolution fusion | flops 1073741824 | bytes 26214400 | tf_op jit(solution)/shard_map/rkb,kbc->rkc/dot_general | solution.py:52
  709.3 8.5 gather_fusion.3
  717.8 13.5 %fusion.27 = bf16[1024,32,128]{2,0,1:T(8,128)(2,1)} fusion(f32[32,128]{1,0:T(8,128)S(1)} %bitcast.137, f32[32,1024,128]{2,1,0:T(8,128)} %fusion.49, bf16[32,1024,128]{2,1,0:T(8,128)(2,1)} %gather_fusion.3, pred[32]{0:T(512)(128)(4,1)S(1)} %get-tuple-element.26, bf16[6,2,32,128,128]{4,3,2,1,0:T(8,128)(2,1)} %param.7), kind=kOutput, calls=%fused_computation.35 | convolution fusion | flops 1094713344 | bytes 34619424 | tf_op jit(solution)/shard_map/rkb,kbc->rkc/dot_general | solution.py:55
  731.3 0.4 collective-permute-start.1
  731.7 11.7 %fusion.46 = f32[32,1024,128]{2,1,0:T(8,128)} fusion(bf16[1024,32,128]{2,0,1:T(8,128)(2,1)} %fusion.27, bf16[6,2,32,128,128]{4,3,2,1,0:T(8,128)(2,1)} %param.7), kind=kOutput, calls=%fused_computation.48 | convolution fusion | flops 1073741824 | bytes 26214400 | tf_op jit(solution)/shard_map/rkb,kbc->rkc/dot_general | solution.py:52
  743.4 1.4 collective-permute-done.1
  744.8 8.8 gather_fusion.4
  753.6 13.5 %fusion.30 = bf16[1024,32,128]{2,0,1:T(8,128)(2,1)} fusion(f32[32,128]{1,0:T(8,128)S(1)} %bitcast.136, f32[32,1024,128]{2,1,0:T(8,128)} %fusion.46, bf16[32,1024,128]{2,1,0:T(8,128)(2,1)} %gather_fusion.4, pred[32]{0:T(512)(128)(4,1)S(1)} %get-tuple-element.34, bf16[6,2,32,128,128]{4,3,2,1,0:T(8,128)(2,1)} %param.7), kind=kOutput, calls=%fused_computation.36 | convolution fusion | flops 1094713344 | bytes 34619424 | tf_op jit(solution)/shard_map/rkb,kbc->rkc/dot_general | solution.py:55
  767.1 11.7 %fusion.43 = f32[32,1024,128]{2,1,0:T(8,128)} fusion(bf16[1024,32,128]{2,0,1:T(8,128)(2,1)} %fusion.30, bf16[6,2,32,128,128]{4,3,2,1,0:T(8,128)(2,1)} %param.7), kind=kOutput, calls=%fused_computation.45 | convolution fusion | flops 1073741824 | bytes 26214400 | tf_op jit(solution)/shard_map/rkb,kbc->rkc/dot_general | solution.py:52
  778.8 0.0 copy-start.1
  778.8 0.0 copy-start.3
  778.8 8.6 gather_fusion.5
  787.4 0.0 copy-done.1
  787.4 0.0 copy-done.3
  787.4 13.7 %fusion.33 = bf16[1024,32,128]{2,0,1:T(8,128)(2,1)} fusion(f32[32,128]{1,0:T(8,128)S(1)} %bitcast.135, f32[32,1024,128]{2,1,0:T(8,128)} %fusion.43, bf16[32,1024,128]{2,1,0:T(8,128)(2,1)} %gather_fusion.5, pred[32]{0:T(512)(128)(4,1)S(1)} %copy-done.3, bf16[6,2,32,128,128]{4,3,2,1,0:T(8,128)(2,1)} %param.7), kind=kOutput, calls=%fused_computation.37 | convolution fusion | flops 1094713344 | bytes 34619424 | tf_op jit(solution)/shard_map/rkb,kbc->rkc/dot_general | solution.py:55
  801.1 12.2 %copy.24 = bf16[1024,32,128]{2,1,0:T(8,128)(2,1)} copy(bf16[1024,32,128]{2,0,1:T(8,128)(2,1)} %fusion.33) | data formatting | bytes 16777216 | tf_op jit(solution)/shard_map/convert_element_type | solution.py:59
  813.3 13.3 %all_to_all.31 = bf16[16,64,4096]{2,1,0:T(8,128)(2,1)} reshape(bf16[1024,32,128]{2,1,0:T(8,128)(2,1)} %copy.24) | data formatting | bytes 16777216 | tf_op jit(solution)/shard_map/all_to_all | solution.py:61
  826.6 231.7 %all_to_all.37 = bf16[16,64,4096]{2,1,0:T(8,128)(2,1)} all-to-all(bf16[16,64,4096]{2,1,0:T(8,128)(2,1)} %all_to_all.31), channel_id=1, replica_groups=mesh['groups'=2,'slab'=16] {'slab'}, dimensions={0} | all-to-all | bytes 16777216 | tf_op jit(solution)/shard_map/all_to_all | solution.py:61
  1058.4 7.9 copy.27
  (3 shorter events, 0.0 us)
Async XLA Ops:
  49.2 8.2 copy-start.2
  49.2 8.7 copy-start
  49.2 305.2 %all-to-all-start = ((bf16[64,16,2,4096]{3,0,2,1:T(8,128)(2,1)}), bf16[64,16,2,4096]{3,0,2,1:T(8,128)(2,1)}, u32[]{:S(2)}, u32[]{:S(2)}) async-start(bf16[64,16,2,4096]{3,0,2,1:T(8,128)(2,1)} %copy.18), calls=%async_computation | async-start | bytes 33554432 | tf_op jit(solution)/shard_map/all_to_all | solution.py:38
  471.9 203.6 %collective-permute-start = (bf16[1024,32,128]{2,0,1:T(8,128)(2,1)}, bf16[1024,32,128]{2,0,1:T(8,128)(2,1)}, u32[]{:S(2)}, u32[]{:S(2)}) collective-permute-start(bf16[1024,32,128]{2,0,1:T(8,128)(2,1)} %fusion.21), channel_id=1, source_target_pairs={{0,2},{2,0},{1,3},{3,1},{4,6},{6,4},{5,7},{7,5},{8,10},{10,8},{9,1... | collective-permute-start | bytes 25165832 | tf_op jit(solution)/shard_map/ppermute | solution.py:16
  731.3 13.5 %collective-permute-start.1 = (bf16[1024,32,128]{2,0,1:T(8,128)(2,1)}, bf16[1024,32,128]{2,0,1:T(8,128)(2,1)}, u32[]{:S(2)}, u32[]{:S(2)}) collective-permute-start(bf16[1024,32,128]{2,0,1:T(8,128)(2,1)} %fusion.27), channel_id=1, source_target_pairs={{0,1},{1,0},{2,3},{3,2},{4,5},{5,4},{6,7},{7,6},{8,9},{9,8},{10,11... | collective-permute-start | bytes 25165832 | tf_op jit(solution)/shard_map/ppermute | solution.py:16
  778.8 8.6 copy-start.1
  778.8 8.6 copy-start.3
where the time goes:
time: 1070 us
  waiting for transfers between devices  466 us (44%)
  blocking collectives  232 us (22%)
  local copies, waits for them, and re-layouts  177 us (17%)
  matrix products  152 us (14%)
  starting transfers between devices  31.4 us (3%)
    all_to_all x1, waiting for transfers between devices, local(): lax.all_to_all(paired, 'slab', split_axis=1, concat_axis=0, tiled=True)  296 us
    all_to_all x1, blocking collectives, local(): lax.all_to_all(flattened, 'slab', split_axis=0, concat_axis=1, tiled=True)  232 us
    ppermute x2, waiting for transfers between devices, from_partner(): return lax.ppermute(block, axis, route)  171 us
    dot_general x6, matrix products, local(): jnp.einsum('rkb,kbc->rkc', crossing, weights[layer_index, 1], preferred_e...  81.4 us
    dot_general x6, matrix products, local(): jnp.einsum('rkb,kbc->rkc', current, weights[layer_index, 0], preferred_el...  70.2 us
    gather x6, local copies, waits for them, and re-layouts, local(): crossing = jnp.take(source, columns[layer_index], axis=1)  51.3 us
    another operation x2, local copies, waits for them, and re-layouts, local(): paired = jnp.stack([grouped, flipped], axis=2)  29.1 us
    ppermute x2, starting transfers between devices, from_partner(): return lax.ppermute(block, axis, route)  23.2 us
  transfers between devices with their start and end apart: 3, of which 3 were waited for; matrix products, arithmetic and copies ran while one was open for 2% of the time, Pallas kernels for 0%

commit v1 on v0

--- a/solution.py
+++ b/solution.py
@@ -58,7 +58,12 @@
         summed = summed + biases[layer_index].reshape(per_device, block_width)
         current = jnp.clip(summed, 0.0, ceiling).astype(jnp.bfloat16)
     flattened = current.reshape(current.shape[0], per_device * block_width)
-    return lax.all_to_all(flattened, "slab", split_axis=0, concat_axis=1, tiled=True)
+    return jnp.concatenate(
+        lax.all_to_all(
+            jnp.stack(jnp.split(flattened, lax.axis_size("slab"), axis=0)), "slab", 0, 0
+        ),
+        axis=1,
+    )
 
 
 def solution(mesh):

time: 1070 us -> 1130 us (1.056)
  local copies, waits for them, and re-layouts: 177 us -> 235 us
    another operation x0 -> x17, local copies, waits for them, and re-layouts: none -> 34.2 us  [local(): jnp.stack(jnp.split(flattened, lax.axis_size('slab'), axis=0))]
    split x0 -> x17, local copies, waits for them, and re-layouts: none -> 33.8 us  [local(): jnp.split(flattened, lax.axis_size('slab'), axis=0)]
    all_to_all x2 -> x0, local copies, waits for them, and re-layouts: 21.2 us -> none  [local(): lax.all_to_all(flattened, 'slab', split_axis=0, concat_axis=1, tiled=True)]
    unnamed x9 -> x50, local copies, waits for them, and re-layouts: 12.2 us -> 27.8 us
    convert_element_type x1 -> x0, local copies, waits for them, and re-layouts: 12.2 us -> none  [local(): current = jnp.clip(summed, 0.0, ceiling).astype(jnp.bfloat16)]
where the time goes in v1:
time: 1130 us; the launch traced here: 1120 us
  waiting for transfers between devices  466 us (41%)
  local copies, waits for them, and re-layouts  235 us (21%)
  blocking collectives  232 us (21%)
  matrix products  151 us (13%)
  starting transfers between devices  31 us (3%)
    all_to_all x1, waiting for transfers between devices, local(): lax.all_to_all(paired, 'slab', split_axis=1, concat_axis=0, tiled=True)  296 us
    all_to_all x1, blocking collectives, local(): lax.all_to_all(jnp.stack(jnp.split(flattened, lax.axis_size('slab'), axis...  232 us
    ppermute x2, waiting for transfers between devices, from_partner(): return lax.ppermute(block, axis, route)  171 us
    dot_general x6, matrix products, local(): jnp.einsum('rkb,kbc->rkc', crossing, weights[layer_index, 1], preferred_e...  81.1 us
    dot_general x6, matrix products, local(): jnp.einsum('rkb,kbc->rkc', current, weights[layer_index, 0], preferred_el...  70.1 us
    gather x6, local copies, waits for them, and re-layouts, local(): crossing = jnp.take(source, columns[layer_index], axis=1)  51.6 us
    another operation x17, local copies, waits for them, and re-layouts, local(): jnp.stack(jnp.split(flattened, lax.axis_size('slab'), axis=0))  34.2 us
    split x17, local copies, waits for them, and re-layouts, local(): jnp.split(flattened, lax.axis_size('slab'), axis=0)  33.8 us
  transfers between devices with their start and end apart: 3, of which 3 were waited for; matrix products, arithmetic and copies ran while one was open for 2% of the time, Pallas kernels for 0%

profile of v1, /device:TPU:1, one launch (start us, length us, event | category | flops | bytes accessed | tf_op | source)
XLA Modules:
  0.0 1124.3 jit_solution(4854934554945823288)
XLA Ops:
  0.0 12.1 %copy.73 = bf16[8,8,16,4096]{3,2,1,0:T(8,128)(2,1)} copy(bf16[8,8,16,4096]{3,1,2,0:T(8,128)(2,1)} %bitcast.134) | data formatting | bytes 16777216
  12.1 7.8 reverse_bitcast_fusion
  19.9 8.0 pad_maximum_fusion
  27.9 21.4 %copy.48 = bf16[64,16,2,4096]{3,0,2,1:T(8,128)(2,1)} copy(bf16[64,16,2,4096]{3,1,0,2:T(8,128)(2,1)S(1)} %pad_maximum_fusion) | data formatting | bytes 33554432 | tf_op jit(solution)/shard_map/stack | solution.py:37
  49.3 7.8 all-to-all-start
  58.4 295.8 %all-to-all-done = bf16[64,16,2,4096]{3,0,2,1:T(8,128)(2,1)} async-done(((bf16[64,16,2,4096]{3,0,2,1:T(8,128)(2,1)}), bf16[64,16,2,4096]{3,0,2,1:T(8,128)(2,1)}, u32[]{:S(2)}, u32[]{:S(2)}) %all-to-all-start) | async-done | bytes 16777248 | tf_op jit(solution)/shard_map/all_to_all | solution.py:38
  354.2 8.3 copy.49
  362.5 6.5 fusion.78
  368.9 12.0 %copy.52 = bf16[1024,1,1,4096]{0,3,2,1:T(8,128)(2,1)} copy(bf16[1024,1,1,4096]{3,0,2,1:T(8,128)(2,1)} %get-tuple-element.18) | data formatting | bytes 16777216 | tf_op jit(solution)/shard_map/slice | solution.py:40
  380.9 11.4 %copy.53 = bf16[1024,32,128]{2,0,1:T(8,128)(2,1)} copy(bf16[1024,32,128]{0,2,1:T(8,128)(2,1)} %bitcast.132) | data formatting | bytes 16777216 | tf_op jit(solution)/shard_map/reshape;squeeze | solution.py:40
  392.3 11.9 %copy.50 = bf16[1024,1,1,4096]{0,3,2,1:T(8,128)(2,1)} copy(bf16[1024,1,1,4096]{3,0,2,1:T(8,128)(2,1)} %get-tuple-element.19) | data formatting | bytes 16777216 | tf_op jit(solution)/shard_map/slice | solution.py:39
  404.3 8.4 gather_fusion
  412.7 11.8 %fusion.58 = f32[32,1024,128]{2,1,0:T(8,128)} fusion(bf16[1024,32,128]{0,2,1:T(8,128)(2,1)} %bitcast.131, bf16[6,2,32,128,128]{4,3,2,1,0:T(8,128)(2,1)} %param.7), kind=kOutput, calls=%fused_computation.60 | convolution fusion | flops 1073741824 | bytes 26214400 | tf_op jit(solution)/shard_map/rkb,kbc->rkc/dot_general | solution.py:52
  424.5 13.5 %fusion.18 = bf16[1024,32,128]{2,0,1:T(8,128)(2,1)} fusion(f32[32,128]{1,0:T(8,128)S(1)} %bitcast.140, f32[32,1024,128]{2,1,0:T(8,128)} %fusion.58, bf16[32,1024,128]{2,1,0:T(8,128)(2,1)} %gather_fusion, pred[32]{0:T(512)(128)(4,1)S(1)} %get-tuple-element.48, bf16[6,2,32,128,128]{4,3,2,1,0:T(8,128)(2,1)} %param.7), kind=kOutput, calls=%fused_computation.32 | convolution fusion | flops 1094713344 | bytes 34619424 | tf_op jit(solution)/shard_map/rkb,kbc->rkc/dot_general | solution.py:55
  438.0 11.7 %fusion.55 = f32[32,1024,128]{2,1,0:T(8,128)} fusion(bf16[1024,32,128]{2,0,1:T(8,128)(2,1)} %fusion.18, bf16[6,2,32,128,128]{4,3,2,1,0:T(8,128)(2,1)} %param.7), kind=kOutput, calls=%fused_computation.57 | convolution fusion | flops 1073741824 | bytes 26214400 | tf_op jit(solution)/shard_map/rkb,kbc->rkc/dot_general | solution.py:52
  449.7 8.4 gather_fusion.1
  458.1 13.7 %fusion.21 = bf16[1024,32,128]{2,0,1:T(8,128)(2,1)} fusion(f32[32,128]{1,0:T(8,128)S(1)} %bitcast.139, f32[32,1024,128]{2,1,0:T(8,128)} %fusion.55, bf16[32,1024,128]{2,1,0:T(8,128)(2,1)} %gather_fusion.1, pred[32]{0:T(512)(128)(4,1)S(1)} %get-tuple-element.46, bf16[6,2,32,128,128]{4,3,2,1,0:T(8,128)(2,1)} %param.7), kind=kOutput, calls=%fused_computation.33 | convolution fusion | flops 1094713344 | bytes 34619424 | tf_op jit(solution)/shard_map/rkb,kbc->rkc/dot_general | solution.py:55
  471.8 22.8 %collective-permute-start = (bf16[1024,32,128]{2,0,1:T(8,128)(2,1)}, bf16[1024,32,128]{2,0,1:T(8,128)(2,1)}, u32[]{:S(2)}, u32[]{:S(2)}) collective-permute-start(bf16[1024,32,128]{2,0,1:T(8,128)(2,1)} %fusion.21), channel_id=1, source_target_pairs={{0,2},{2,0},{1,3},{3,1},{4,6},{6,4},{5,7},{7,5},{8,10},{10,8},{9,1... | collective-permute-start | bytes 25165832 | tf_op jit(solution)/shard_map/ppermute | solution.py:16
  494.6 11.7 %fusion.52 = f32[32,1024,128]{2,1,0:T(8,128)} fusion(bf16[1024,32,128]{2,0,1:T(8,128)(2,1)} %fusion.21, bf16[6,2,32,128,128]{4,3,2,1,0:T(8,128)(2,1)} %param.7), kind=kOutput, calls=%fused_computation.54 | convolution fusion | flops 1073741824 | bytes 26214400 | tf_op jit(solution)/shard_map/rkb,kbc->rkc/dot_general | solution.py:52
  506.3 169.1 %collective-permute-done = bf16[1024,32,128]{2,0,1:T(8,128)(2,1)} collective-permute-done((bf16[1024,32,128]{2,0,1:T(8,128)(2,1)}, bf16[1024,32,128]{2,0,1:T(8,128)(2,1)}, u32[]{:S(2)}, u32[]{:S(2)}) %collective-permute-start) | collective-permute-done | bytes 8388640 | tf_op jit(solution)/shard_map/ppermute | solution.py:16
  675.4 8.6 gather_fusion.2
  684.0 13.5 %fusion.24 = bf16[1024,32,128]{2,0,1:T(8,128)(2,1)} fusion(f32[32,128]{1,0:T(8,128)S(1)} %bitcast.138, f32[32,1024,128]{2,1,0:T(8,128)} %fusion.52, bf16[32,1024,128]{2,1,0:T(8,128)(2,1)} %gather_fusion.2, pred[32]{0:T(512)(128)(4,1)S(1)} %get-tuple-element.44, bf16[6,2,32,128,128]{4,3,2,1,0:T(8,128)(2,1)} %param.7), kind=kOutput, calls=%fused_computation.34 | convolution fusion | flops 1094713344 | bytes 34619424 | tf_op jit(solution)/shard_map/rkb,kbc->rkc/dot_general | solution.py:55
  697.5 11.7 %fusion.49 = f32[32,1024,128]{2,1,0:T(8,128)} fusion(bf16[1024,32,128]{2,0,1:T(8,128)(2,1)} %fusion.24, bf16[6,2,32,128,128]{4,3,2,1,0:T(8,128)(2,1)} %param.7), kind=kOutput, calls=%fused_computation.51 | convolution fusion | flops 1073741824 | bytes 26214400 | tf_op jit(solution)/shard_map/rkb,kbc->rkc/dot_general | solution.py:52
  709.1 8.5 gather_fusion.3
  717.7 13.5 %fusion.27 = bf16[1024,32,128]{2,0,1:T(8,128)(2,1)} fusion(f32[32,128]{1,0:T(8,128)S(1)} %bitcast.137, f32[32,1024,128]{2,1,0:T(8,128)} %fusion.49, bf16[32,1024,128]{2,1,0:T(8,128)(2,1)} %gather_fusion.3, pred[32]{0:T(512)(128)(4,1)S(1)} %get-tuple-element.42, bf16[6,2,32,128,128]{4,3,2,1,0:T(8,128)(2,1)} %param.7), kind=kOutput, calls=%fused_computation.35 | convolution fusion | flops 1094713344 | bytes 34619424 | tf_op jit(solution)/shard_map/rkb,kbc->rkc/dot_general | solution.py:55
  731.6 11.7 %fusion.46 = f32[32,1024,128]{2,1,0:T(8,128)} fusion(bf16[1024,32,128]{2,0,1:T(8,128)(2,1)} %fusion.27, bf16[6,2,32,128,128]{4,3,2,1,0:T(8,128)(2,1)} %param.7), kind=kOutput, calls=%fused_computation.48 | convolution fusion | flops 1073741824 | bytes 26214400 | tf_op jit(solution)/shard_map/rkb,kbc->rkc/dot_general | solution.py:52
  743.2 1.5 collective-permute-done.1
  744.7 9.0 gather_fusion.4
  753.6 13.5 %fusion.30 = bf16[1024,32,128]{2,0,1:T(8,128)(2,1)} fusion(f32[32,128]{1,0:T(8,128)S(1)} %bitcast.136, f32[32,1024,128]{2,1,0:T(8,128)} %fusion.46, bf16[32,1024,128]{2,1,0:T(8,128)(2,1)} %gather_fusion.4, pred[32]{0:T(512)(128)(4,1)S(1)} %get-tuple-element.50, bf16[6,2,32,128,128]{4,3,2,1,0:T(8,128)(2,1)} %param.7), kind=kOutput, calls=%fused_computation.36 | convolution fusion | flops 1094713344 | bytes 34619424 | tf_op jit(solution)/shard_map/rkb,kbc->rkc/dot_general | solution.py:55
  767.1 11.7 %fusion.43 = f32[32,1024,128]{2,1,0:T(8,128)} fusion(bf16[1024,32,128]{2,0,1:T(8,128)(2,1)} %fusion.30, bf16[6,2,32,128,128]{4,3,2,1,0:T(8,128)(2,1)} %param.7), kind=kOutput, calls=%fused_computation.45 | convolution fusion | flops 1073741824 | bytes 26214400 | tf_op jit(solution)/shard_map/rkb,kbc->rkc/dot_general | solution.py:52
  778.8 8.6 gather_fusion.5
  787.4 13.5 %fusion.33 = bf16[1024,32,128]{2,0,1:T(8,128)(2,1)} fusion(f32[32,128]{1,0:T(8,128)S(1)} %bitcast.135, f32[32,1024,128]{2,1,0:T(8,128)} %fusion.43, bf16[32,1024,128]{2,1,0:T(8,128)(2,1)} %gather_fusion.5, pred[32]{0:T(512)(128)(4,1)S(1)} %copy-done.16, bf16[6,2,32,128,128]{4,3,2,1,0:T(8,128)(2,1)} %param.7), kind=kOutput, calls=%fused_computation.37 | convolution fusion | flops 1094713344 | bytes 34619424 | tf_op jit(solution)/shard_map/rkb,kbc->rkc/dot_general | solution.py:55
  800.8 6.1 fusion.79
  808.1 2.1 stack.55
  810.1 1.9 constant_dynamic-update-slice_fusion.15
  812.0 2.2 copy.55
  814.2 2.1 stack.56
  816.3 2.2 copy.56
  818.4 2.1 stack.57
  820.5 2.2 copy.57
  822.7 2.1 stack.58
  824.8 2.2 copy.58
  826.9 2.1 stack.59
  829.0 2.2 copy.59
  831.2 2.1 stack.60
  833.2 2.2 copy.60
  835.4 2.1 stack.61
  837.5 2.2 copy.61
  839.7 2.1 stack.62
  841.7 2.2 copy.62
  843.9 2.1 stack.63
  846.0 2.2 copy.63
  848.2 2.1 stack.64
  851.4 2.1 stack.65
  854.6 2.1 stack.66
  857.9 2.1 stack.67
  861.1 2.1 stack.68
  864.4 2.1 stack.69
  866.5 1.2 copy.69
  867.7 2.1 stack.70
  873.2 1.9 constant_dynamic-update-slice_fusion.10
  875.9 1.9 constant_dynamic-update-slice_fusion.8
  884.5 231.8 %all_to_all.23 = bf16[16,64,4096]{2,1,0:T(8,128)(2,1)} all-to-all(bf16[16,64,4096]{2,1,0:T(8,128)(2,1)} %constant_dynamic-update-slice_fusion), channel_id=1, replica_groups=mesh['groups'=2,'slab'=16] {'slab'}, dimensions={0} | all-to-all | bytes 16777216 | tf_op jit(solution)/shard_map/all_to_all | solution.py:62
  1116.2 7.9 copy.72
  (59 shorter events, 19.4 us)
Async XLA Ops:
  49.3 7.8 copy-start.15
  49.3 8.4 copy-start.13
  49.3 304.9 %all-to-all-start = ((bf16[64,16,2,4096]{3,0,2,1:T(8,128)(2,1)}), bf16[64,16,2,4096]{3,0,2,1:T(8,128)(2,1)}, u32[]{:S(2)}, u32[]{:S(2)}) async-start(bf16[64,16,2,4096]{3,0,2,1:T(8,128)(2,1)} %copy.48), calls=%async_computation | async-start | bytes 33554432 | tf_op jit(solution)/shard_map/all_to_all | solution.py:38
  471.8 203.6 %collective-permute-start = (bf16[1024,32,128]{2,0,1:T(8,128)(2,1)}, bf16[1024,32,128]{2,0,1:T(8,128)(2,1)}, u32[]{:S(2)}, u32[]{:S(2)}) collective-permute-start(bf16[1024,32,128]{2,0,1:T(8,128)(2,1)} %fusion.21), channel_id=1, source_target_pairs={{0,2},{2,0},{1,3},{3,1},{4,6},{6,4},{5,7},{7,5},{8,10},{10,8},{9,1... | collective-permute-start | bytes 25165832 | tf_op jit(solution)/shard_map/ppermute | solution.py:16
  731.1 13.5 %collective-permute-start.1 = (bf16[1024,32,128]{2,0,1:T(8,128)(2,1)}, bf16[1024,32,128]{2,0,1:T(8,128)(2,1)}, u32[]{:S(2)}, u32[]{:S(2)}) collective-permute-start(bf16[1024,32,128]{2,0,1:T(8,128)(2,1)} %fusion.27), channel_id=1, source_target_pairs={{0,1},{1,0},{2,3},{3,2},{4,5},{5,4},{6,7},{7,6},{8,9},{9,8},{10,11... | collective-permute-start | bytes 25165832 | tf_op jit(solution)/shard_map/ppermute | solution.py:16
  778.8 8.6 copy-start.14
  778.8 8.6 copy-start.16
  851.4 18.5 %copy-start = (bf16[1,64,4096]{2,1,0:T(8,128)(2,1)S(1)}, bf16[1,64,4096]{2,1,0:T(8,128)(2,1)}, u32[]{:S(2)}) copy-start(bf16[1,64,4096]{2,1,0:T(8,128)(2,1)} %stack.56) | copy-start | bytes 1572868
  854.6 16.1 %copy-start.1 = (bf16[1,64,4096]{2,1,0:T(8,128)(2,1)S(1)}, bf16[1,64,4096]{2,1,0:T(8,128)(2,1)}, u32[]{:S(2)}) copy-start(bf16[1,64,4096]{2,1,0:T(8,128)(2,1)} %stack.57) | copy-start | bytes 1572868
  857.9 13.7 %copy-start.2 = (bf16[1,64,4096]{2,1,0:T(8,128)(2,1)S(1)}, bf16[1,64,4096]{2,1,0:T(8,128)(2,1)}, u32[]{:S(2)}) copy-start(bf16[1,64,4096]{2,1,0:T(8,128)(2,1)} %stack.58) | copy-start | bytes 1572868
  861.1 11.2 %copy-start.3 = (bf16[1,64,4096]{2,1,0:T(8,128)(2,1)S(1)}, bf16[1,64,4096]{2,1,0:T(8,128)(2,1)}, u32[]{:S(2)}) copy-start(bf16[1,64,4096]{2,1,0:T(8,128)(2,1)} %stack.59) | copy-start | bytes 1572868
  864.4 10.7 copy-start.4
  867.7 10.1 copy-start.5
  869.8 8.8 copy-start.6
  869.8 9.6 copy-start.7
  869.8 10.4 copy-start.8
  869.9 11.3 %copy-start.9 = (bf16[1,64,4096]{2,1,0:T(8,128)(2,1)S(1)}, bf16[1,64,4096]{2,1,0:T(8,128)(2,1)}, u32[]{:S(2)}) copy-start(bf16[1,64,4096]{2,1,0:T(8,128)(2,1)} %stack.67) | copy-start | bytes 1572868
  869.9 12.1 %copy-start.10 = (bf16[1,64,4096]{2,1,0:T(8,128)(2,1)S(1)}, bf16[1,64,4096]{2,1,0:T(8,128)(2,1)}, u32[]{:S(2)}) copy-start(bf16[1,64,4096]{2,1,0:T(8,128)(2,1)} %stack.68) | copy-start | bytes 1572868
  869.9 12.9 %copy-start.11 = (bf16[1,64,4096]{2,1,0:T(8,128)(2,1)S(1)}, bf16[1,64,4096]{2,1,0:T(8,128)(2,1)}, u32[]{:S(2)}) copy-start(bf16[1,64,4096]{2,1,0:T(8,128)(2,1)} %stack.69) | copy-start | bytes 1572868
  869.9 13.7 %copy-start.12 = (bf16[1,64,4096]{2,1,0:T(8,128)(2,1)S(1)}, bf16[1,64,4096]{2,1,0:T(8,128)(2,1)}, u32[]{:S(2)}) copy-start(bf16[1,64,4096]{2,1,0:T(8,128)(2,1)} %stack.70) | copy-start | bytes 1572868
